TPU v7x, 128 devices: a whole 4x4x4 slice. The times are simulated.
128 devices in a mesh: req: 4 (over z_lo, core), seq: 32 (over y, x, z_hi).
Axes of the slice: x: 4, y: 4, z: 4 (z_hi: 2, z_lo: 2; z = z_hi * 2 + z_lo), core: 2. Of those that a mesh axis runs over, the one named last changes fastest.
Arguments:
- prefill_query: bfloat16 [16384, 1536], P(('req', 'seq')), may hold values from -512 to 512
- prefill_key: bfloat16 [16384, 512], P(('req', 'seq')), may hold values from -512 to 512
- prefill_value: bfloat16 [16384, 512], P(('req', 'seq')), may hold values from -6 to 6
- prefill_resid: bfloat16 [16384, 1536], P(('req', 'seq')), may hold values from -6 to 6
- dec_query: bfloat16 [16, 1536], P('req'), may hold values from -512 to 512
- dec_key_new: bfloat16 [16, 512], P('req'), may hold values from -16 to 16
- dec_value_new: bfloat16 [16, 512], P('req'), may hold values from -6 to 6
- dec_resid: bfloat16 [16, 1536], P('req'), may hold values from -6 to 6
- cache_lengths: int32 [16], P('req'), may hold values from 16 to 32768, as said below
- key_cache: bfloat16 [16, 32768, 512], P('req', 'seq'), may hold values from -512 to 512
- value_cache: bfloat16 [16, 32768, 512], P('req', 'seq'), may hold values from -6 to 6
- attn_out_weight: bfloat16 [1536, 1536], replicated, may hold values from -0.15625 to 0.15625
- ffn_gain: float32 [1536], replicated, may hold values from 0.1 to 1.9
- expert_gate: bfloat16 [32, 1536, 512], P('seq', 'req'), may hold values from -0.15625 to 0.15625
- expert_up: bfloat16 [32, 1536, 512], P('seq', 'req'), may hold values from -0.15625 to 0.15625
- expert_down: bfloat16 [32, 512, 1536], P('seq', None, 'req'), may hold values from -0.25 to 0.25
- routes: int32 [16384, 8], P(('req', 'seq')), may hold values from 0 to 31, all different within a row; in each aligned block of 128 rows (0 to 127, 128 to 255, ...) at most 40 rows name the same one
- route_weights: float32 [16384, 8], P(('req', 'seq')), may hold values from 0.05 to 0.5
Outputs:
- prefill_out: bfloat16 [16384, 1536], P(('req', 'seq'))
- dec_out: bfloat16 [16, 1536], P('req')
Inputs may be any that keep to these rules, and one draw needn't show every extreme that they name: `routes`: in each aligned block of 128 rows (the rows of one device) no expert is named by more than 40 rows. `cache_lengths`: some request uses all 32768 positions.
All inputs are finite; a program needn't handle non-finite values.
Results may differ from a plain program's by a relative error of at most 0.012.
Values may be sent and summed in bfloat16 or wider, within the bound.
No kernel may reach another device: no remote copies, remote signals or barrier semaphores. Data moves between devices by JAX's collectives and lax.ppermute only.
A program may use at most 128 MiB of HBM per device.

v0:
```python
import math
import jax
import jax.numpy as jnp
from jax import lax
from jax.sharding import PartitionSpec as P

D = 1536
HEADS = 24
KVH = 8
HD = 64
EXPERTS = 32
CAP = 40
NEGATIVE = -1e30
EPSILON = 1e-05


def rms_scale(hidden, gain):
    values_float = hidden.astype(jnp.float32)
    mean_square = jnp.mean(values_float * values_float, axis=-1, keepdims=True)
    return (values_float * lax.rsqrt(mean_square + EPSILON) * gain).astype(jnp.bfloat16)


def per_request(function, operands):
    return jax.vmap(function)(operands)


def prefill_attention(prefill_query, prefill_key, prefill_value):
    token_rows = prefill_query.shape[0]
    group_size = HEADS // KVH
    score_scale = 1.0 / math.sqrt(HD)
    own_start = lax.axis_index("seq") * token_rows
    query_position = own_start + jnp.arange(token_rows, dtype=jnp.int32)
    query_heads = prefill_query.reshape(token_rows, KVH, group_size, HD)
    initial = (
        jnp.full((KVH, group_size, token_rows), NEGATIVE, jnp.float32),
        jnp.zeros((KVH, group_size, token_rows), jnp.float32),
        jnp.zeros((token_rows, KVH, group_size, HD), jnp.float32),
    )
    key_rows = lax.all_gather(prefill_key, "seq", axis=0, tiled=True)
    value_rows = lax.all_gather(prefill_value, "seq", axis=0, tiled=True)
    key_count = key_rows.shape[0]
    block_rows = 512
    key_heads = key_rows.reshape(key_count, KVH, HD)
    value_heads = value_rows.reshape(key_count, KVH, HD)

    def add_block(number, running_state):
        maxima, totals, weighted = running_state
        offset = number * block_rows
        key_block = lax.dynamic_slice_in_dim(key_heads, offset, block_rows, 0)
        value_block = lax.dynamic_slice_in_dim(value_heads, offset, block_rows, 0)
        key_position = offset + jnp.arange(block_rows, dtype=jnp.int32)
        visible = (key_position[None, :] <= query_position[:, None])[None, None, :, :]
        logits = (
            jnp.einsum("qkgd,pkd->kgqp", query_heads, key_block, preferred_element_type=jnp.float32)
            * score_scale
        )
        logits = jnp.where(visible, logits, NEGATIVE)
        new_maxima = jnp.maximum(maxima, jnp.max(logits, axis=-1))
        exponent = jnp.where(visible, jnp.exp(logits - new_maxima[..., None]), 0.0)
        rescale = jnp.exp(maxima - new_maxima)
        totals = totals * rescale + jnp.sum(exponent, axis=-1)
        weighted = weighted * jnp.moveaxis(rescale, 2, 0)[..., None] + jnp.einsum(
            "kgqp,pkd->qkgd",
            exponent.astype(jnp.bfloat16),
            value_block,
            preferred_element_type=jnp.float32,
        )
        return (new_maxima, totals, weighted)

    maxima, totals, weighted = lax.fori_loop(0, key_count // block_rows, add_block, initial)
    return (
        (weighted / jnp.moveaxis(totals, 2, 0)[..., None])
        .reshape(token_rows, HEADS * HD)
        .astype(jnp.bfloat16)
    )


def decode_attention(dec_query, dec_key_new, dec_value_new, cache_lengths, key_cache, value_cache):
    requests, block_length, feature_width = key_cache.shape
    group_size = HEADS // KVH
    score_scale = 1.0 / math.sqrt(HD)
    first_position = lax.axis_index("seq") * block_length
    positions = first_position + jnp.arange(block_length, dtype=jnp.int32)
    valid_mask = positions[None, :] < cache_lengths[:, None]
    query_heads = dec_query.reshape(requests, KVH, group_size, HD)
    key_heads = key_cache.reshape(requests, block_length, KVH, HD)
    value_heads = value_cache.reshape(requests, block_length, KVH, HD)

    def scores_of(pieces):
        query_one, keys_one, valid_one = pieces
        logits = (
            jnp.einsum("kgd,pkd->kgp", query_one, keys_one, preferred_element_type=jnp.float32)
            * score_scale
        )
        return jnp.where(valid_one[None, None, :], logits, NEGATIVE)

    def terms_of(pieces):
        scores_one, maxima_one, values_one, valid_one = pieces
        exponent = jnp.where(
            valid_one[None, None, :], jnp.exp(scores_one - maxima_one[..., None]), 0.0
        )
        weighted_one = jnp.einsum(
            "kgp,pkd->kgd",
            exponent.astype(jnp.bfloat16),
            values_one,
            preferred_element_type=jnp.float32,
        )
        return (jnp.sum(exponent, axis=-1), weighted_one)

    scores = per_request(scores_of, (query_heads, key_heads, valid_mask))
    local_maxima = jnp.max(scores, axis=-1)
    maxima = lax.pmax(local_maxima, "seq")
    totals, weighted = per_request(terms_of, (scores, maxima, value_heads, valid_mask))
    totals, weighted = lax.psum((totals, weighted), "seq")
    fresh_score = (
        jnp.einsum(
            "rkgd,rkd->rkg",
            query_heads,
            dec_key_new.reshape(requests, KVH, HD),
            preferred_element_type=jnp.float32,
        )
        * score_scale
    )
    final_maxima = jnp.maximum(maxima, fresh_score)
    rescale = jnp.exp(maxima - final_maxima)
    fresh_exp = jnp.exp(fresh_score - final_maxima)
    denominator = totals * rescale + fresh_exp
    fresh_weight = lax.optimization_barrier(fresh_exp.astype(jnp.bfloat16)).astype(jnp.float32)
    numerator = weighted * rescale[..., None] + fresh_weight[..., None] * dec_value_new.reshape(
        requests, KVH, 1, HD
    ).astype(jnp.float32)
    return (numerator / denominator[..., None]).reshape(requests, HEADS * HD).astype(jnp.bfloat16)


def expert_rows(rows_batch, gate_full, up_full, down_full):
    gate_value = jnp.einsum(
        "erd,edf->erf", rows_batch, gate_full, preferred_element_type=jnp.float32
    )
    up_value = jnp.einsum("erd,edf->erf", rows_batch, up_full, preferred_element_type=jnp.float32)
    hidden = (jax.nn.silu(gate_value) * up_value).astype(jnp.bfloat16)
    return jnp.einsum("erf,efd->erd", hidden, down_full, preferred_element_type=jnp.float32).astype(
        jnp.bfloat16
    )


def body(
    prefill_query,
    prefill_key,
    prefill_value,
    prefill_resid,
    dec_query,
    dec_key_new,
    dec_value_new,
    dec_resid,
    cache_lengths,
    key_cache,
    value_cache,
    attn_out_weight,
    ffn_gain,
    expert_gate,
    expert_up,
    expert_down,
    routes,
    route_weights,
):
    attended = prefill_attention(prefill_query, prefill_key, prefill_value)
    middle = (
        prefill_resid.astype(jnp.float32)
        + jnp.dot(attended, attn_out_weight, preferred_element_type=jnp.float32)
    ).astype(jnp.bfloat16)
    normed = rms_scale(middle, ffn_gain)
    gate_full, up_full = (
        lax.all_gather(expert_gate, "req", axis=1, tiled=True),
        lax.all_gather(expert_up, "req", axis=1, tiled=True),
    )
    down_full = lax.all_gather(expert_down, "req", axis=2, tiled=True)
    token_rows, top_count = routes.shape
    flat_expert = routes.reshape(-1)
    token_index = jnp.arange(token_rows * top_count, dtype=jnp.int32) // top_count
    onehot = (flat_expert[:, None] == jnp.arange(EXPERTS, dtype=jnp.int32)[None, :]).astype(
        jnp.int32
    )
    earlier = jnp.cumsum(onehot, axis=0) - onehot
    slot_index = jnp.sum(earlier * onehot, axis=1)
    outgoing = (
        jnp.zeros((EXPERTS, CAP, D), jnp.bfloat16)
        .at[flat_expert, slot_index]
        .set(normed[token_index])
    )
    incoming = lax.all_to_all(outgoing[:, None], "seq", split_axis=0, concat_axis=1, tiled=True)
    local_experts, sources, slot_count, feature_width = incoming.shape
    result = expert_rows(
        incoming.reshape(local_experts, sources * slot_count, feature_width),
        gate_full,
        up_full,
        down_full,
    )
    result = result.reshape(local_experts, sources, slot_count, feature_width)
    returned = lax.all_to_all(result, "seq", split_axis=1, concat_axis=0, tiled=True)
    picked = returned.reshape(EXPERTS, CAP, D)[flat_expert, slot_index]
    picked = picked.reshape(token_rows, top_count, D)
    mixture = jnp.sum(route_weights[..., None] * picked.astype(jnp.float32), axis=1)
    prefill_out = (middle.astype(jnp.float32) + mixture).astype(jnp.bfloat16)
    decoded = decode_attention(
        dec_query, dec_key_new, dec_value_new, cache_lengths, key_cache, value_cache
    )
    dec_out = (
        dec_resid.astype(jnp.float32)
        + jnp.dot(decoded, attn_out_weight, preferred_element_type=jnp.float32)
    ).astype(jnp.bfloat16)
    return (prefill_out, dec_out)


def solution(mesh):
    return jax.shard_map(
        body,
        mesh=mesh,
        in_specs=(
            P(("req", "seq"), None),
            P(("req", "seq"), None),
            P(("req", "seq"), None),
            P(("req", "seq"), None),
            P("req", None),
            P("req", None),
            P("req", None),
            P("req", None),
            P("req"),
            P("req", "seq", None),
            P("req", "seq", None),
            P(),
            P(),
            P("seq", "req", None),
            P("seq", "req", None),
            P("seq", None, "req"),
            P(("req", "seq"), None),
            P(("req", "seq"), None),
        ),
        out_specs=(P(("req", "seq"), None), P("req", None)),
        check_vma=False,
    )
```

profile of v0, /device:TPU:0, one launch (start us, length us, event | category | flops | bytes accessed | tf_op | source)
XLA Modules:
  0.0 821.3 jit_solution(3442623777327935929)
XLA Ops:
  11.1 1.2 copy.41
  12.3 9.0 %reduce-window.6 = s32[32,8,128]{2,1,0:T(8,128)S(1)} reduce-window(s32[32,8,128]{2,1,0:T(8,128)S(1)} %fusion.51, s32[]{:T(128)} %constant.93.clone.1), window={size=1x1x128 pad=0_0x0_0x127_0}, to_apply=%region_4.5 | reduce-window | flops 4161536 | bytes 262148 | tf_op jit(solution)/shard_map/reduce-window
  23.4 72.7 %all-gather.6.cloned.1.call-done = bf16[4096,512]{1,0:T(8,128)(2,1)} async-done(((bf16[128,512]{1,0:T(8,128)(2,1)}), bf16[4096,512]{1,0:T(8,128)(2,1)}) %all-gather.6.cloned.1.call-update) | async-done | bytes 4194320 | tf_op jit(solution)/shard_map/all_gather | solution.py:39
  96.1 6.4 copy.40
  102.5 75.9 %all-gather.8.cloned.1.call-done = bf16[4096,512]{1,0:T(8,128)(2,1)} async-done(((bf16[128,512]{1,0:T(8,128)(2,1)}), bf16[4096,512]{1,0:T(8,128)(2,1)}) %all-gather.8.cloned.1.call-update) | async-done | bytes 4194320 | tf_op jit(solution)/shard_map/all_gather | solution.py:40
  178.4 6.4 copy.42
  184.8 98.8 %while.18 = (s32[]{:T(128)}, f32[8,3,128]{2,1,0:T(4,128)S(1)}, f32[8,3,128]{2,1,0:T(4,128)S(1)}, f32[128,8,3,64]{0,3,2,1:T(8,128)S(1)}, bf16[4096,8,64]{0,2,1:T(...) while((s32[]{:T(128)}, f32[8,3,128]{2,1,0:T(4,128)S(1)}, ...), condition=%wide.region_3.4_spmd.clone, body=%wide.region_0.3_spmd.clone.sunk | while | flops 423774848 | bytes 47518944 | solution.py:70
  185.0 4.8 fusion.83
  189.8 4.5 fusion.85
  194.5 2.8 fusion.87
  197.5 4.8 fusion.83
  202.3 4.4 fusion.85
  206.9 2.8 fusion.87
  209.8 4.8 fusion.83
  214.6 4.4 fusion.85
  219.2 2.8 fusion.87
  222.2 4.8 fusion.83
  227.0 4.4 fusion.85
  231.6 2.8 fusion.87
  234.5 4.8 fusion.83
  239.3 4.4 fusion.85
  243.9 2.8 fusion.87
  246.8 4.8 fusion.83
  251.6 4.4 fusion.85
  256.2 2.8 fusion.87
  259.2 4.8 fusion.83
  263.9 4.4 fusion.85
  268.5 2.8 fusion.87
  271.5 4.8 fusion.83
  276.3 4.4 fusion.85
  280.8 2.8 fusion.87
  283.7 3.2 multiply_reduce_fusion
  287.0 0.9 copy-done.1
  288.0 18.6 %scatter_custom_fusion = bf16[1280,1536]{1,0:T(8,128)(2,1)} fusion(s32[1024]{0:T(1024)S(1)} %get-tuple-element.207, bf16[128,1536]{1,0:T(8,128)(2,1)S(1)} %multiply_convert_fusion, s32[1024]{0:T(1024)S(1)} %get-tuple-element.206, bf16[]{:T(256)} %constant.98.clone.1), kind=kCustom, calls=%fused_computation.36 | custom fusion | bytes 3932162
  306.7 5.1 all-to-all-start
  312.4 52.8 %all-to-all-done = bf16[32,1,40,1536]{3,2,1,0:T(8,128)(2,1)} async-done(((bf16[32,1,40,1536]{3,2,1,0:T(8,128)(2,1)}), bf16[32,1,40,1536]{3,2,1,0:T(8,128)(2,1)}, u32[]{:S(2)}, u32[]{:S(2)}) %all-to-all-start) | async-done | bytes 3932192 | tf_op jit(solution)/shard_map/all_to_all | solution.py:190
  365.2 4.8 fusion.36
  370.1 9.5 %convolution_convert_fusion = bf16[1280,1536]{1,0:T(8,128)(2,1)} fusion(bf16[1,512,1536]{2,1,0:T(8,128)(2,1)} %all-gather.14.cloned.1.call-done, bf16[1280,1536]{1,0:T(8,128)(2,1)} %bitcast.10, f32[1280,512]{1,0:T(8,128)S(1)} %fusion.36, bf16[1,1536,512]{2,1,0:T(8,128)(2,1)} %all-gather.12.cloned.1.call-done), kind=kOutput, calls=%fused_computation.32 | convolution fusion | flops 4032430080 | bytes 13631488 | tf_op jit(solution)/shard_map/erf,efd->erd/dot_general | solution.py:141
  379.5 7.5 all-to-all-start.1
  387.2 6.3 copy.51
  393.7 6.3 copy.50
  400.2 2.9 fusion.58
  403.2 205.7 %pmax.7 = f32[4,8,3]{2,1,0:T(8,128)S(1)} all-reduce(f32[4,8,3]{2,1,0:T(8,128)S(1)} %get-tuple-element.204), channel_id=1, replica_groups=mesh['req'=4,'seq'=32] {'seq'}, use_global_device_ids=true, to_apply=%region_11.12 | all-reduce | flops 96 | bytes 768 | tf_op jit(solution)/shard_map/pmax | solution.py:112
  609.3 3.5 fusion.43
  612.7 176.5 %all-reduce = (f32[4,8,3,64]{3,2,1,0:T(4,128)S(1)}, f32[4,8,3]{2,1,0:T(8,128)S(1)}) all-reduce(f32[4,8,3,64]{3,2,1,0:T(4,128)S(1)} %fusion.43, f32[4,8,3]{2,1,0:T(8,128)S(1)} %fusion.41), channel_id=1, replica_groups=mesh['req'=4,'seq'=32] {'seq'}, use_global_device_ids=true, to_apply=%region_12.13 | all-reduce | flops 6240 | bytes 49920 | tf_op jit(solution)/shard_map/psum | solution.py:114
  789.7 3.7 fusion.32
  793.4 17.8 %gather_fusion = bf16[1024,1536]{1,0:T(8,128)(2,1)S(1)} fusion(bf16[32,40,1536]{2,1,0:T(8,128)(2,1)} %bitcast.16, s32[1024]{0:T(1024)S(1)} %bitcast.111), kind=kCustom, calls=%fused_computation.1 | custom fusion | bytes 6299648 | tf_op jit(solution)/shard_map/gather | solution.py:200
  811.2 2.8 fusion.26
  (133 shorter events, 11.4 us)
Async XLA Ops:
  7.2 88.9 %all-gather.6.cloned.1.call-start = ((), (), s32[]{:S(2)}) async-start(), calls=%async_computation.2 | async-start | bytes 4325376 | tf_op jit(solution)/shard_map/all_gather | solution.py:39
  7.9 170.5 %all-gather.8.cloned.1.call-start = ((), (), s32[]{:S(2)}) async-start(), calls=%async_computation.3 | async-start | bytes 4325376 | tf_op jit(solution)/shard_map/all_gather | solution.py:40
  8.6 303.7 %all-gather.10.cloned.1.call-start = ((), (), s32[]{:S(2)}) async-start(), calls=%async_computation.4 | async-start | bytes 1966080 | tf_op jit(solution)/shard_map/all_gather | solution.py:173
  9.4 360.7 %all-gather.14.cloned.1.call-start = ((), (), s32[]{:S(2)}) async-start(), calls=%async_computation.6 | async-start | bytes 1966080 | tf_op jit(solution)/shard_map/all_gather | solution.py:176
  184.8 98.9 %copy-start.3 = (bf16[128,1536]{1,0:T(8,128)(2,1)S(1)}, bf16[128,1536]{1,0:T(8,128)(2,1)}, u32[]{:S(2)}) copy-start(bf16[128,1536]{1,0:T(8,128)(2,1)} %param.23) | copy-start | bytes 1179652
  189.8 4.7 copy-start
  202.3 4.6 copy-start
  214.6 4.6 copy-start
  227.0 4.6 copy-start
  239.3 4.6 copy-start
  251.6 4.6 copy-start
  263.9 4.6 copy-start
  276.2 4.6 copy-start
  283.6 4.3 copy-start.6
  287.0 0.9 copy-start.1
  306.7 58.5 %all-to-all-start = ((bf16[32,1,40,1536]{3,2,1,0:T(8,128)(2,1)}), bf16[32,1,40,1536]{3,2,1,0:T(8,128)(2,1)}, u32[]{:S(2)}, u32[]{:S(2)}) async-start(bf16[32,1,40,1536]{3,2,1,0:T(8,128)(2,1)} %bitcast.114), calls=%async_computation | async-start | bytes 7864320 | tf_op jit(solution)/shard_map/all_to_all | solution.py:190
  311.8 58.3 %all-gather.12.cloned.1.call-start = ((), (), s32[]{:S(2)}) async-start(), calls=%async_computation.5 | async-start | bytes 1966080 | tf_op jit(solution)/shard_map/all_gather | solution.py:174
  379.5 7.6 copy-start.7
  379.5 413.8 %all-to-all-start.1 = ((bf16[1,32,40,1536]{3,2,0,1:T(8,128)(2,1)}), bf16[1,32,40,1536]{3,2,0,1:T(8,128)(2,1)}, u32[]{:S(2)}, u32[]{:S(2)}) async-start(bf16[1,32,40,1536]{3,2,0,1:T(8,128)(2,1)} %bitcast.118), calls=%async_computation.1 | async-start | bytes 7864320 | tf_op jit(solution)/shard_map/all_to_all | solution.py:199
  387.2 6.3 copy-start.4
  393.6 6.4 copy-start.8
  393.6 6.4 copy-start.9
  393.7 6.5 copy-start.10
  403.2 386.5 %copy-start.5 = (bf16[4,1536]{1,0:T(4,128)(2,1)S(1)}, bf16[4,1536]{1,0:T(4,128)(2,1)}, u32[]{:S(2)}) copy-start(bf16[4,1536]{1,0:T(4,128)(2,1)} %param.27) | copy-start | bytes 36868
  811.2 2.8 copy-start.2
Sparse Core Ops, SparseCore 0:
  11.0 85.0 all-gather.5
  99.1 79.3 all-gather.7
  180.1 21.5 all-gather.9
  203.2 25.7 all-gather.13
  313.9 54.2 all-gather.11
where the time goes:
time: 823 us; the launch traced here: 821 us
  blocking collectives  382 us (46%)
  waiting for transfers between devices  204 us (25%)
  matrix products  88 us (11%)
  local copies, waits for them, and re-layouts  67 us (8%)
  other arithmetic  52 us (6%)
  between operations  14.1 us (2%)
  starting transfers between devices  13 us (2%)
    pmax x1, blocking collectives, decode_attention(): maxima = lax.pmax(local_maxima, 'seq')  206 us
    psum x1, blocking collectives, decode_attention(): totals, weighted = lax.psum((totals, weighted), 'seq')  176 us
    all_gather x1, waiting for transfers between devices, prefill_attention(): value_rows = lax.all_gather(prefill_value, 'seq', axis=0, tiled=True)  75.9 us
    all_gather x1, waiting for transfers between devices, prefill_attention(): key_rows = lax.all_gather(prefill_key, 'seq', axis=0, tiled=True)  72.7 us
    all_to_all x1, waiting for transfers between devices, body(): lax.all_to_all(outgoing[:, None], 'seq', split_axis=0, concat_axis=1, til...  52.8 us
    dot_general x8, matrix products, add_block(): jnp.einsum('qkgd,pkd->kgqp', query_heads, key_block, preferred_element_ty...  38.2 us
    reduce_sum x8, other arithmetic, add_block(): totals = totals * rescale + jnp.sum(exponent, axis=-1)  35.4 us
    unnamed x26, local copies, waits for them, and re-layouts  34.3 us
  transfers between devices with their start and end apart: 7, of which 3 were waited for; matrix products, arithmetic and copies ran while one was open for 21% of the time, Pallas kernels for 0%

commit v1 on v0

--- a/solution.py
+++ b/solution.py
@@ -36,8 +36,13 @@
         jnp.zeros((KVH, group_size, token_rows), jnp.float32),
         jnp.zeros((token_rows, KVH, group_size, HD), jnp.float32),
     )
-    key_rows = lax.all_gather(prefill_key, "seq", axis=0, tiled=True)
-    value_rows = lax.all_gather(prefill_value, "seq", axis=0, tiled=True)
+    key_rows, value_rows = jnp.split(
+        lax.all_gather(
+            jnp.concatenate([prefill_key, prefill_value], axis=1), "seq", axis=0, tiled=True
+        ),
+        [prefill_key.shape[1]],
+        axis=1,
+    )
     key_count = key_rows.shape[0]
     block_rows = 512
     key_heads = key_rows.reshape(key_count, KVH, HD)

time: 823 us -> 771 us (0.937)
  waiting for transfers between devices: 204 us -> 152 us
  other arithmetic: 52 us -> 30.3 us
  matrix products: 88 us -> 105 us
    all_gather x2 -> x1, waiting for transfers between devices: 149 us -> 95.4 us  [prefill_attention(): lax.all_gather(jnp.concatenate([prefill_key, prefill_value], axis=1), 'se...]
    reduce_sum x8, other arithmetic: 35.4 us -> 11.8 us  [add_block(): totals = totals * rescale + jnp.sum(exponent, axis=-1)]
    split x0 -> x3, local copies, waits for them, and re-layouts: none -> 18.7 us  [prefill_attention(): jnp.split(lax.all_gather(jnp.concatenate([prefill_key, prefill_value], ax...]
    dot_general x8, matrix products: 22.1 us -> 39 us  [add_block(): jnp.einsum('kgqp,pkd->qkgd', exponent.astype(jnp.bfloat16), value_block,...]
    all_gather x2 -> x0, local copies, waits for them, and re-layouts: 12.8 us -> none  [the longest x1 6.43 us: prefill_attention(): key_rows = lax.all_gather(prefill_key, 'seq', axis=0, tiled=True)]
  transfers between devices with their start and end apart: 7 -> 6, of which waited for: 3 -> 2; matrix products, arithmetic and copies ran while one was open for 21% -> 23% of each run, Pallas kernels for 0% -> 0%
where the time goes in v1:
time: 771 us; the launch traced here: 769 us
  blocking collectives  383 us (50%)
  waiting for transfers between devices  152 us (20%)
  matrix products  105 us (14%)
  local copies, waits for them, and re-layouts  71.9 us (9%)
  other arithmetic  30.3 us (4%)
  between operations  14 us (2%)
  starting transfers between devices  11.8 us (2%)
    pmax x1, blocking collectives, decode_attention(): maxima = lax.pmax(local_maxima, 'seq')  207 us
    psum x1, blocking collectives, decode_attention(): totals, weighted = lax.psum((totals, weighted), 'seq')  176 us
    all_gather x1, waiting for transfers between devices, prefill_attention(): lax.all_gather(jnp.concatenate([prefill_key, prefill_value], axis=1), 'se...  95.4 us
    all_to_all x1, waiting for transfers between devices, body(): lax.all_to_all(outgoing[:, None], 'seq', split_axis=0, concat_axis=1, til...  55.3 us
    dot_general x8, matrix products, add_block(): jnp.einsum('kgqp,pkd->qkgd', exponent.astype(jnp.bfloat16), value_block,...  39 us
    dot_general x8, matrix products, add_block(): jnp.einsum('qkgd,pkd->kgqp', query_heads, key_block, preferred_element_ty...  38.1 us
    unnamed x26, local copies, waits for them, and re-layouts  34.3 us
    split x3, local copies, waits for them, and re-layouts, prefill_attention(): jnp.split(lax.all_gather(jnp.concatenate([prefill_key, prefill_value], ax...  18.7 us
  transfers between devices with their start and end apart: 6, of which 2 were waited for; matrix products, arithmetic and copies ran while one was open for 23% of the time, Pallas kernels for 0%

profile of v1, /device:TPU:0, one launch (start us, length us, event | category | flops | bytes accessed | tf_op | source)
XLA Modules:
  0.0 769.1 jit_solution(16025975133880410723)
XLA Ops:
  7.2 1.7 pad_maximum_fusion
  11.6 9.0 %reduce-window.6 = s32[32,8,128]{2,1,0:T(8,128)S(1)} reduce-window(s32[32,8,128]{2,1,0:T(8,128)S(1)} %fusion.51, s32[]{:T(128)} %constant.93.clone.1), window={size=1x1x128 pad=0_0x0_0x127_0}, to_apply=%region_4.5 | reduce-window | flops 4161536 | bytes 262148 | tf_op jit(solution)/shard_map/reduce-window
  22.6 1.2 copy.41
  23.8 95.4 %all-gather.5.cloned.1.call-done = bf16[4096,1024]{1,0:T(8,128)(2,1)} async-done(((bf16[128,1024]{1,0:T(8,128)(2,1)}), bf16[4096,1024]{1,0:T(8,128)(2,1)}) %all-gather.5.cloned.1.call-update) | async-done | bytes 8388624 | tf_op jit(solution)/shard_map/all_gather | solution.py:40
  119.2 5.8 fusion.58
  125.0 6.4 copy.40
  131.5 6.5 copy.42
  138.0 91.1 %while.18 = (s32[]{:T(128)}, f32[8,3,128]{2,1,0:T(4,128)S(1)}, f32[8,3,128]{2,1,0:T(4,128)S(1)}, f32[128,8,3,64]{0,3,2,1:T(8,128)S(1)}, bf16[4096,8,64]{0,2,1:T(...) while((s32[]{:T(128)}, f32[8,3,128]{2,1,0:T(4,128)S(1)}, ...), condition=%wide.region_3.4_spmd.clone, body=%wide.region_0.3_spmd.clone.sunk | while | flops 423774848 | bytes 47518936 | solution.py:75
  138.1 4.8 fusion.84
  142.9 4.8 fusion.88
  147.8 1.5 fusion.86
  149.5 4.8 fusion.84
  154.3 5.1 fusion.88
  159.4 1.5 fusion.86
  161.1 4.8 fusion.84
  165.9 4.9 fusion.88
  170.8 1.5 fusion.86
  172.5 4.8 fusion.84
  177.3 4.8 fusion.88
  182.1 1.5 fusion.86
  183.8 4.8 fusion.84
  188.6 4.8 fusion.88
  193.5 1.5 fusion.86
  195.2 4.8 fusion.84
  200.0 4.8 fusion.88
  204.8 1.5 fusion.86
  206.5 4.8 fusion.84
  211.3 4.8 fusion.88
  216.2 1.5 fusion.86
  217.9 4.8 fusion.84
  222.6 4.8 fusion.88
  227.5 1.5 fusion.86
  229.1 3.2 multiply_reduce_fusion
  233.4 18.6 %scatter_custom_fusion = bf16[1280,1536]{1,0:T(8,128)(2,1)} fusion(s32[1024]{0:T(1024)S(1)} %get-tuple-element.209, bf16[128,1536]{1,0:T(8,128)(2,1)S(1)} %multiply_convert_fusion, s32[1024]{0:T(1024)S(1)} %get-tuple-element.208, bf16[]{:T(256)} %constant.98.clone.1), kind=kCustom, calls=%fused_computation.36 | custom fusion | bytes 3932162
  252.0 5.7 all-to-all-start
  258.3 55.3 %all-to-all-done = bf16[32,1,40,1536]{3,2,1,0:T(8,128)(2,1)} async-done(((bf16[32,1,40,1536]{3,2,1,0:T(8,128)(2,1)}), bf16[32,1,40,1536]{3,2,1,0:T(8,128)(2,1)}, u32[]{:S(2)}, u32[]{:S(2)}) %all-to-all-start) | async-done | bytes 3932192 | tf_op jit(solution)/shard_map/all_to_all | solution.py:195
  313.6 4.8 fusion.36
  318.5 9.4 %convolution_convert_fusion = bf16[1280,1536]{1,0:T(8,128)(2,1)} fusion(bf16[1,512,1536]{2,1,0:T(8,128)(2,1)} %all-gather.11.cloned.1.call-done, bf16[1280,1536]{1,0:T(8,128)(2,1)} %bitcast.10, f32[1280,512]{1,0:T(8,128)S(1)} %fusion.36, bf16[1,1536,512]{2,1,0:T(8,128)(2,1)} %all-gather.9.cloned.1.call-done), kind=kOutput, calls=%fused_computation.32 | convolution fusion | flops 4032430080 | bytes 13631488 | tf_op jit(solution)/shard_map/erf,efd->erd/dot_general | solution.py:146
  327.9 5.8 all-to-all-start.1
  333.7 6.3 copy.50
  340.1 6.4 copy.51
  346.6 2.9 fusion.59
  349.6 206.9 %pmax.7 = f32[4,8,3]{2,1,0:T(8,128)S(1)} all-reduce(f32[4,8,3]{2,1,0:T(8,128)S(1)} %get-tuple-element.206), channel_id=1, replica_groups=mesh['req'=4,'seq'=32] {'seq'}, use_global_device_ids=true, to_apply=%region_11.12 | all-reduce | flops 96 | bytes 768 | tf_op jit(solution)/shard_map/pmax | solution.py:117
  556.9 3.4 fusion.43
  560.3 176.5 %all-reduce = (f32[4,8,3,64]{3,2,1,0:T(4,128)S(1)}, f32[4,8,3]{2,1,0:T(8,128)S(1)}) all-reduce(f32[4,8,3,64]{3,2,1,0:T(4,128)S(1)} %fusion.43, f32[4,8,3]{2,1,0:T(8,128)S(1)} %fusion.41), channel_id=1, replica_groups=mesh['req'=4,'seq'=32] {'seq'}, use_global_device_ids=true, to_apply=%region_12.13 | all-reduce | flops 6240 | bytes 49920 | tf_op jit(solution)/shard_map/psum | solution.py:119
  737.4 3.7 fusion.32
  741.1 17.8 %gather_fusion = bf16[1024,1536]{1,0:T(8,128)(2,1)S(1)} fusion(bf16[32,40,1536]{2,1,0:T(8,128)(2,1)} %bitcast.16, s32[1024]{0:T(1024)S(1)} %bitcast.111), kind=kCustom, calls=%fused_computation.1 | custom fusion | bytes 6299648 | tf_op jit(solution)/shard_map/gather | solution.py:205
  758.9 2.8 fusion.26
  (132 shorter events, 10.0 us)
Async XLA Ops:
  7.2 112.1 %all-gather.5.cloned.1.call-start = ((), (), s32[]{:S(2)}) async-start(), calls=%async_computation.2 | async-start | bytes 8650752 | tf_op jit(solution)/shard_map/all_gather | solution.py:40
  8.9 249.4 %all-gather.7.cloned.1.call-start = ((), (), s32[]{:S(2)}) async-start(), calls=%async_computation.3 | async-start | bytes 1966080 | tf_op jit(solution)/shard_map/all_gather | solution.py:178
  9.7 308.7 %all-gather.11.cloned.1.call-start = ((), (), s32[]{:S(2)}) async-start(), calls=%async_computation.5 | async-start | bytes 1966080 | tf_op jit(solution)/shard_map/all_gather | solution.py:181
  138.0 91.2 %copy-start.3 = (bf16[128,1536]{1,0:T(8,128)(2,1)S(1)}, bf16[128,1536]{1,0:T(8,128)(2,1)}, u32[]{:S(2)}) copy-start(bf16[128,1536]{1,0:T(8,128)(2,1)} %param.23) | copy-start | bytes 1179652
  142.9 4.9 copy-start
  154.2 5.2 copy-start
  165.9 4.9 copy-start
  177.3 4.9 copy-start
  188.6 4.9 copy-start
  200.0 4.9 copy-start
  211.3 4.9 copy-start
  222.6 4.9 copy-start
  229.0 4.2 copy-start.6
  232.4 0.9 copy-start.1
  252.0 61.6 %all-to-all-start = ((bf16[32,1,40,1536]{3,2,1,0:T(8,128)(2,1)}), bf16[32,1,40,1536]{3,2,1,0:T(8,128)(2,1)}, u32[]{:S(2)}, u32[]{:S(2)}) async-start(bf16[32,1,40,1536]{3,2,1,0:T(8,128)(2,1)} %bitcast.114), calls=%async_computation | async-start | bytes 7864320 | tf_op jit(solution)/shard_map/all_to_all | solution.py:195
  257.7 60.7 %all-gather.9.cloned.1.call-start = ((), (), s32[]{:S(2)}) async-start(), calls=%async_computation.4 | async-start | bytes 1966080 | tf_op jit(solution)/shard_map/all_gather | solution.py:179
  327.9 5.8 copy-start.4
  327.9 413.2 %all-to-all-start.1 = ((bf16[1,32,40,1536]{3,2,0,1:T(8,128)(2,1)}), bf16[1,32,40,1536]{3,2,0,1:T(8,128)(2,1)}, u32[]{:S(2)}, u32[]{:S(2)}) async-start(bf16[1,32,40,1536]{3,2,0,1:T(8,128)(2,1)} %bitcast.118), calls=%async_computation.1 | async-start | bytes 7864320 | tf_op jit(solution)/shard_map/all_to_all | solution.py:204
  340.1 6.4 copy-start.7
  340.1 6.4 copy-start.10
  349.6 387.4 %copy-start.8 = (bf16[4,512]{1,0:T(4,128)(2,1)S(1)}, bf16[4,512]{1,0:T(4,128)(2,1)}, u32[]{:S(2)}) copy-start(bf16[4,512]{1,0:T(4,128)(2,1)} %param.26) | copy-start | bytes 12292
  349.6 387.8 %copy-start.9 = (f32[128,8]{0,1:T(8,128)S(1)}, f32[128,8]{0,1:T(8,128)}, u32[]{:S(2)}) copy-start(f32[128,8]{0,1:T(8,128)} %param.37) | copy-start | bytes 12292
  349.6 387.9 %copy-start.5 = (bf16[4,1536]{1,0:T(4,128)(2,1)S(1)}, bf16[4,1536]{1,0:T(4,128)(2,1)}, u32[]{:S(2)}) copy-start(bf16[4,1536]{1,0:T(4,128)(2,1)} %param.27) | copy-start | bytes 36868
  758.9 2.9 copy-start.2
Sparse Core Ops, SparseCore 0:
  11.6 107.5 all-gather.4
  120.9 22.4 all-gather.6
  145.1 25.7 all-gather.10
  259.9 54.0 all-gather.8
